TPU v7x, 32 devices: a whole 2x2x4 slice. The times are simulated.
32 devices in a mesh: row: 4 (over y, x), col: 8 (over z, core).
Axes of the slice: x: 2, y: 2, z: 4, core: 2. Of those that a mesh axis runs over, the one named last changes fastest.
Arguments:
- sim: bfloat16 [8192, 8192], P('row', 'col'), may hold values from -6 to 6
- diag_blocks: bfloat16 [2048, 8192], P(None, 'col'), may hold values from -0.125 to 0.125
- match_perm: int32 [4, 2048], replicated, may hold values from 0 to 2047, each once within a row
- match_scale: float32 [4, 2048], replicated, may hold values from 0.3 to 1.5
- features: bfloat16 [8192, 256], P('col'), may hold values from -0.0625 to 0.0625
Outputs:
- new_sim: bfloat16 [8192, 8192], P('row', 'col')
- aggregated: float32 [8192, 256], P(('row', 'col'))
Inputs may be any that keep to these rules, and one draw needn't show every extreme that they name: Each row of match_perm lists every number of 0 to 2047 once.
All inputs are finite; a program needn't handle non-finite values.
Results may differ from a plain program's by a relative error of at most 0.0058.
Values may be sent and summed in bfloat16 or wider, within the bound.
No kernel may reach another device: no remote copies, remote signals or barrier semaphores. Data moves between devices by JAX's collectives and lax.ppermute only.
A program may use at most 128 MiB of HBM per device.

v0:
```python
import jax
import jax.numpy as jnp
from jax import lax
from jax.sharding import PartitionSpec as P

decay_factor = 0.8


def partner_2(value, axis, bit):
    mask = 2**bit
    pairs = [(source, source ^ mask) for source in range(lax.axis_size(axis))]
    return lax.ppermute(value, axis, pairs)


def shifted(value, axis, steps):
    count = lax.axis_size(axis)
    pairs = [(source, (source + steps) % count) for source in range(count)]
    return lax.ppermute(value, axis, pairs)


def spread(x, axis, root):
    mine = lax.axis_index(axis) == root
    return lax.psum(jnp.where(mine, x, jnp.zeros_like(x)), axis)


def on_device(sim, diag_blocks, match_perm, match_scale, features):
    row_count = lax.axis_size("row")
    col_count = lax.axis_size("col")
    blocks_here = col_count // 2 // row_count
    row_id = lax.axis_index("row")
    col_id = lax.axis_index("col")
    block_id = col_id // 2
    side = col_id % 2
    half_width = sim.shape[1]
    tile_rows = sim.shape[0]
    partner = partner_2(sim, "col", 0)
    first_half = jnp.where(side == 0, sim, partner)
    second_half = jnp.where(side == 0, partner, sim)
    whole_block = jnp.concatenate([first_half, second_half], axis=1)
    perm_block = lax.dynamic_index_in_dim(match_perm, block_id, 0, keepdims=False)
    scale_block = lax.dynamic_index_in_dim(match_scale, block_id, 0, keepdims=False)
    own_perm = lax.dynamic_slice_in_dim(perm_block, side * half_width, half_width, 0)
    own_scale = lax.dynamic_slice_in_dim(scale_block, side * half_width, half_width, 0)
    moved_cols = (jnp.take(whole_block, own_perm, axis=1) * own_scale[None, :]).astype(jnp.bfloat16)
    arrived_cols = shifted(moved_cols, "col", col_count // 2)
    mixed = (
        jnp.dot(whole_block, diag_blocks, preferred_element_type=jnp.float32) + arrived_cols
    ).astype(jnp.bfloat16)
    position = 0
    source = row_id * blocks_here + position
    perm_rows = lax.dynamic_index_in_dim(match_perm, source, 0, keepdims=False)
    scale_rows = lax.dynamic_index_in_dim(match_scale, source, 0, keepdims=False)
    sent_rows = (jnp.take(mixed, perm_rows, axis=0) * scale_rows[:, None]).astype(jnp.bfloat16)
    arrived_rows = shifted(sent_rows, "row", row_count // 2)
    position = 0
    target = row_id * blocks_here + position
    halves = []
    for part in range(2):
        left_half = spread(diag_blocks, "col", 2 * target + part)
        halves.append(
            lax.dot_general(
                left_half, mixed, (((0,), (0,)), ((), ())), preferred_element_type=jnp.float32
            )
        )
    product = jnp.concatenate(halves, axis=0)
    results = decay_factor * (product + arrived_rows)
    global_rows = row_id * tile_rows + lax.broadcasted_iota(jnp.int32, results.shape, 0)
    global_cols = col_id * half_width + lax.broadcasted_iota(jnp.int32, results.shape, 1)
    new_sim = jnp.where(global_rows == global_cols, 1.0, results).astype(jnp.bfloat16)
    partial_value = jnp.dot(new_sim, features, preferred_element_type=jnp.float32)
    aggregated = lax.psum_scatter(partial_value, "col", scatter_dimension=0, tiled=True)
    return (new_sim, aggregated)


def solution(mesh):
    placed = (P("row", "col"), P(None, "col"), P(), P(), P("col", None))
    return jax.shard_map(
        on_device,
        mesh=mesh,
        in_specs=placed,
        out_specs=(P("row", "col"), P(("row", "col"), None)),
        check_vma=False,
    )
```

profile of v0, /device:TPU:0, one launch (start us, length us, event | category | flops | bytes accessed | tf_op | source)
XLA Modules:
  0.0 503.9 jit_solution(8184790162820065224)
XLA Ops:
  7.2 0.0 copy-start
  7.2 0.0 all-reduce.3.cloned.1.call-start
  7.2 6.5 %copy.12 = bf16[2048,1024]{0,1:T(8,128)(2,1)} copy(bf16[2048,1024]{1,0:T(8,128)(2,1)} %param.5) | data formatting | bytes 8388608 | tf_op args[0]
  13.7 0.5 collective-permute-start
  14.2 0.8 dynamic_slice.23
  15.0 0.8 compare_select_fusion.1
  15.8 5.5 %collective-permute-done = bf16[2048,1024]{0,1:T(8,128)(2,1)} collective-permute-done((bf16[2048,1024]{0,1:T(8,128)(2,1)}, bf16[2048,1024]{0,1:T(8,128)(2,1)}, u32[]{:S(2)}, u32[]{:S(2)}) %collective-permute-start) | collective-permute-done | bytes 4194336 | tf_op jit(solution)/shard_map/ppermute | solution.py:12
  21.3 5.7 %broadcast_select_fusion.2 = (bf16[2048,1024]{0,1:T(8,128)(2,1)}, bf16[2048,1024]{0,1:T(8,128)(2,1)}) fusion(bf16[2048,1024]{0,1:T(8,128)(2,1)} %copy.12, bf16[2048,1024]{0,1:T(8,128)(2,1)} %collective-permute-done, pred[]{:T(512)S(6)} %eq.17), kind=kLoop, calls=%fused_computation.13 | loop fusion | flops 4194304 | bytes 16777216 | tf_op jit(solution)/shard_map/jit(_where)/select_n | solution.py:37
  27.0 8.4 %pad_maximum_fusion = bf16[2048,2048]{0,1:T(8,128)(2,1)} fusion(bf16[2048,1024]{0,1:T(8,128)(2,1)} %get-tuple-element.9, bf16[2048,1024]{0,1:T(8,128)(2,1)} %get-tuple-element.8), kind=kLoop, calls=%fused_computation.2 | loop fusion | flops 16777216 | bytes 16777216 | tf_op jit(solution)/shard_map/concatenate | solution.py:39
  35.4 13.3 %gather_fusion = bf16[1024,2048]{1,0:T(8,128)(2,1)} fusion(bf16[2048,2048]{0,1:T(8,128)(2,1)} %pad_maximum_fusion, s32[1024]{0:T(1024)S(1)} %broadcast_clamp_fusion.1), kind=kCustom, calls=%fused_computation | custom fusion | bytes 8392704 | tf_op jit(solution)/shard_map/jit(_take)/gather | solution.py:44
  48.7 6.4 %copy.14 = bf16[1024,2048]{0,1:T(8,128)(2,1)} copy(bf16[1024,2048]{1,0:T(8,128)(2,1)} %gather_fusion) | data formatting | bytes 8388608 | tf_op jit(solution)/shard_map/jit(_take)/gather | solution.py:44
  55.1 5.4 %fusion.3 = bf16[2048,1024]{1,0:T(8,128)(2,1)} fusion(f32[1024]{0:T(1024)S(1)} %bitcast.22, bf16[1024,2048]{0,1:T(8,128)(2,1)} %copy.14, pred[1024]{0:T(1024)(128)(4,1)S(1)} %compare_and_fusion.1), kind=kLoop, calls=%fused_computation.10 | loop fusion | flops 8388608 | bytes 8393728 | tf_op jit(solution)/shard_map/convert_element_type | solution.py:44
  60.4 3.9 collective-permute-start.1
  64.4 6.0 %broadcast_select_fusion.3 = (bf16[2048,1024]{1,0:T(8,128)(2,1)}, bf16[2048,1024]{1,0:T(8,128)(2,1)}) fusion(bf16[2048,1024]{1,0:T(8,128)(2,1)} %param.6, pred[]{:T(512)S(6)} %eq.16, pred[]{:T(512)S(6)} %eq.18), kind=kLoop, calls=%fused_computation.14 | loop fusion | flops 4194304 | bytes 12582914 | tf_op jit(solution)/shard_map/jit(_where)/select_n | solution.py:23
  70.4 0.0 all-reduce.3.cloned.1.call-update
  70.5 0.2 reduce-scatter.2.cloned.1.call-start
  70.7 0.8 constant_dynamic-slice_fusion
  71.5 0.8 compare_select_fusion
  72.3 251.8 %collective-permute-done.1 = bf16[2048,1024]{1,0:T(8,128)(2,1)} collective-permute-done((bf16[2048,1024]{1,0:T(8,128)(2,1)}, bf16[2048,1024]{1,0:T(8,128)(2,1)}, u32[]{:S(2)}, u32[]{:S(2)}) %collective-permute-start.1) | collective-permute-done | bytes 4194336 | tf_op jit(solution)/shard_map/ppermute | solution.py:18
  324.1 14.7 %add_convert_fusion = bf16[2048,1024]{1,0:T(8,128)(2,1)} fusion(bf16[2048,1024]{1,0:T(8,128)(2,1)} %collective-permute-done.1, bf16[2048,1024]{1,0:T(8,128)(2,1)} %param.6, bf16[2048,1024]{0,1:T(8,128)(2,1)} %get-tuple-element.9, bf16[2048,1024]{0,1:T(8,128)(2,1)} %get-tuple-element.8), kind=kOutput, calls=%fused_computation.9 | convolution fusion | flops 8613003264 | bytes 20971520 | tf_op jit(solution)/shard_map/dot_general | solution.py:47
  338.8 13.7 %gather_fusion.1 = bf16[2048,1024]{1,0:T(8,128)(2,1)} fusion(bf16[2048,1024]{1,0:T(8,128)(2,1)} %add_convert_fusion, s32[2048]{0:T(1024)S(1)} %broadcast_clamp_fusion), kind=kCustom, calls=%fused_computation.1 | custom fusion | bytes 8396800 | tf_op jit(solution)/shard_map/jit(_take)/gather | solution.py:53
  352.5 4.2 multiply_convert_fusion.1
  356.7 1.6 collective-permute-start.2
  358.3 44.8 %all-reduce.3.cloned.1.call-done = (bf16[2048,1024]{1,0:T(8,128)(2,1)}, bf16[2048,1024]{1,0:T(8,128)(2,1)}) async-done(((bf16[2048,1024]{1,0:T(8,128)(2,1)}, bf16[2048,1024]{1,0:T(8,128)(2,1)}), (bf16[2048,1024]{1,0:T(8,128)(2,1)}, bf16[2048,1024]{1,0:T(8,128)(2,1)})) %all-reduce.3.cloned.1.call-update) | async-done | bytes 8388624 | tf_op jit(solution)/shard_map/psum | solution.py:23
  403.1 0.0 copy-start.1
  403.1 0.0 copy-start.3
  403.2 7.9 %fusion.4 = f32[1024,1024]{1,0:T(8,128)S(1)} fusion(bf16[2048,1024]{1,0:T(8,128)(2,1)} %get-tuple-element.3, bf16[2048,1024]{1,0:T(8,128)(2,1)} %add_convert_fusion), kind=kOutput, calls=%fused_computation.27 | convolution fusion | flops 4294967296 | bytes 12582912 | tf_op jit(solution)/shard_map/dot_general | solution.py:61
  411.1 0.0 copy-done.1
  411.1 0.0 copy-done.3
  411.1 4.6 fusion.5
  415.8 33.4 %collective-permute-done.2 = bf16[2048,1024]{1,0:T(8,128)(2,1)} collective-permute-done((bf16[2048,1024]{1,0:T(8,128)(2,1)}, bf16[2048,1024]{1,0:T(8,128)(2,1)}, u32[]{:S(2)}, u32[]{:S(2)}) %collective-permute-start.2) | collective-permute-done | bytes 4194336 | tf_op jit(solution)/shard_map/ppermute | solution.py:18
  449.1 4.1 fusion.2
  453.3 0.0 copy-start.2
  453.3 2.0 copy-done.2
  455.3 0.0 copy-done
  455.3 2.6 fusion.6
  457.9 0.0 reduce-scatter.2.cloned.1.call-update
  457.9 39.2 %reduce-scatter.2.cloned.1.call-done = f32[256,256]{1,0:T(8,128)} async-done(((f32[2048,256]{1,0:T(8,128)}), f32[256,256]{1,0:T(8,128)}) %reduce-scatter.2.cloned.1.call-update) | async-done | bytes 262160 | tf_op jit(solution)/shard_map/reduce_scatter | solution.py:71
  (6 shorter events, 0.0 us)
Async XLA Ops:
  7.2 448.1 %copy-start = (bf16[1024,256]{1,0:T(8,128)(2,1)S(1)}, bf16[1024,256]{1,0:T(8,128)(2,1)}, u32[]{:S(2)}) copy-start(bf16[1024,256]{1,0:T(8,128)(2,1)} %param.9) | copy-start | bytes 1572868
  7.2 396.0 %all-reduce.3.cloned.1.call-start = ((), (), s32[]{:S(2)}) async-start(), calls=%async_computation.2 | async-start | bytes 16777216 | tf_op jit(solution)/shard_map/psum | solution.py:23
  13.7 7.6 %collective-permute-start = (bf16[2048,1024]{0,1:T(8,128)(2,1)}, bf16[2048,1024]{0,1:T(8,128)(2,1)}, u32[]{:S(2)}, u32[]{:S(2)}) collective-permute-start(bf16[2048,1024]{0,1:T(8,128)(2,1)} %copy.12), channel_id=1, source_target_pairs={{0,1},{1,0},{2,3},{3,2},{4,5},{5,4},{6,7},{7,6},{8,9},{9,8},{10,11... | collective-permute-start | bytes 12582920 | tf_op jit(solution)/shard_map/ppermute | solution.py:12
  60.4 263.7 %collective-permute-start.1 = (bf16[2048,1024]{1,0:T(8,128)(2,1)}, bf16[2048,1024]{1,0:T(8,128)(2,1)}, u32[]{:S(2)}, u32[]{:S(2)}) collective-permute-start(bf16[2048,1024]{1,0:T(8,128)(2,1)} %fusion.3), channel_id=1, source_target_pairs={{0,4},{1,5},{2,6},{3,7},{4,0},{5,1},{6,2},{7,3},{8,12},{9,13},{10,... | collective-permute-start | bytes 12582920 | tf_op jit(solution)/shard_map/ppermute | solution.py:18
  70.5 426.6 %reduce-scatter.2.cloned.1.call-start = ((), (), s32[]{:S(2)}) async-start(), calls=%async_computation.1 | async-start | bytes 2359296 | tf_op jit(solution)/shard_map/reduce_scatter | solution.py:71
  356.7 92.5 %collective-permute-start.2 = (bf16[2048,1024]{1,0:T(8,128)(2,1)}, bf16[2048,1024]{1,0:T(8,128)(2,1)}, u32[]{:S(2)}, u32[]{:S(2)}) collective-permute-start(bf16[2048,1024]{1,0:T(8,128)(2,1)} %multiply_convert_fusion.1), channel_id=1, source_target_pairs={{0,16},{8,24},{16,0},{24,8},{1,17},{9,25},{17,1},{25,9},{2,18},{10... | collective-permute-start | bytes 12582920 | tf_op jit(solution)/shard_map/ppermute | solution.py:18
  403.1 8.0 %copy-start.1 = (bf16[2048,1024]{1,0:T(8,128)(2,1)S(1)}, bf16[2048,1024]{1,0:T(8,128)(2,1)}, u32[]{:S(2)}) copy-start(bf16[2048,1024]{1,0:T(8,128)(2,1)} %add_convert_fusion) | copy-start | bytes 12582916
  403.1 8.0 %copy-start.3 = (bf16[2048,1024]{1,0:T(8,128)(2,1)S(1)}, bf16[2048,1024]{1,0:T(8,128)(2,1)}, u32[]{:S(2)}) copy-start(bf16[2048,1024]{1,0:T(8,128)(2,1)} %get-tuple-element.2) | copy-start | bytes 12582916
  453.3 2.0 copy-start.2
Sparse Core Ops, SparseCore 0:
  70.6 332.5 all-reduce.2
  458.0 38.9 reduce-scatter.1
where the time goes:
time: 505 us; the launch traced here: 504 us
  waiting for transfers between devices  375 us (74%)
  local copies, waits for them, and re-layouts  43.5 us (9%)
  other arithmetic  35.4 us (7%)
  matrix products  29.8 us (6%)
  between operations  14.1 us (3%)
  starting transfers between devices  6.31 us (1%)
    ppermute x2, waiting for transfers between devices, shifted(): return lax.ppermute(value, axis, pairs)  285 us
    psum x1, waiting for transfers between devices, spread(): return lax.psum(jnp.where(mine, x, jnp.zeros_like(x)), axis)  44.8 us
    reduce_scatter x1, waiting for transfers between devices, on_device(): lax.psum_scatter(partial_value, 'col', scatter_dimension=0, tiled=True)  39.2 us
    gather x2, local copies, waits for them, and re-layouts, on_device(): jnp.take(whole_block, own_perm, axis=1) * own_scale[None, :]  19.7 us
    dot_general x1, matrix products, on_device(): jnp.dot(whole_block, diag_blocks, preferred_element_type=jnp.float32)  14.7 us
    gather x1, local copies, waits for them, and re-layouts, on_device(): jnp.take(mixed, perm_rows, axis=0) * scale_rows[:, None]  13.7 us
    dot_general x2, matrix products, on_device(): lax.dot_general(left_half, mixed, (((0,), (0,)), ((), ())), preferred_ele...  12.6 us
  transfers between devices with their start and end apart: 5, of which 5 were waited for; matrix products, arithmetic and copies ran while one was open for 11% of the time, Pallas kernels for 0%

commit v1 on v0

v1 whole, which is shorter than its diff:
```python
import jax
import jax.numpy as jnp
from jax import lax
from jax.experimental import pallas as pl
from jax.experimental.pallas import tpu as pltpu
from jax.sharding import PartitionSpec as P


decay_factor = 0.8
parts = (2, 2, 2, 2, 2, 2, 2, 1, 1)
groups = ((0, 4), (4, 6))


def flipped(value, axis, mask):
    pairs = [(source, source ^ mask) for source in range(lax.axis_size(axis))]
    return lax.ppermute(value, axis, pairs)


def shifted(value, axis, steps):
    count = lax.axis_size(axis)
    pairs = [(source, (source + steps) % count) for source in range(count)]
    return lax.ppermute(value, axis, pairs)


def dot(a, b):
    return jnp.dot(a, b, preferred_element_type=jnp.float32)


def dot_t(a, b):
    return lax.dot_general(a, b, (((0,), (0,)), ((), ())), preferred_element_type=jnp.float32)


def one_hot(start, rows, targets):
    index = start + lax.broadcasted_iota(jnp.int32, (rows, targets.shape[0]), 0)
    return (index == targets[None, :]).astype(jnp.bfloat16)


def part(x, start, size, axis=0):
    return lax.dynamic_slice_in_dim(x, start, size, axis)


def pick(items, index):
    result = items[0]
    for position in range(1, len(items)):
        result = jnp.where(index == position, items[position], result)
    return result


def tile_product(refs, kept, h, start):
    b_own, b_par, perm, scale = refs
    near, far = kept
    shape = (perm.shape[1], near.shape[0])
    index = start + lax.broadcasted_iota(jnp.int32, shape, 1)
    chosen = (index == perm[0]).astype(jnp.bfloat16)
    moved = dot(chosen, far[...]) * scale[0]
    return moved + dot_t(jnp.where(h == 0, b_own[...], b_par[...]), near[...])


def keep(chunks, kept):
    @pl.when((pl.program_id(0) == 0) & (pl.program_id(1) == 0))
    def _():
        start = 0
        for pair in chunks:
            depth = pair[0].shape[0]
            for one, whole in zip(pair, kept):
                whole[start : start + depth] = one[...]
            start += depth


def tile_specs(start, depth, chunks, tile, tiles, at):
    wide = chunks[0][0].shape[1]
    last = at(tiles - 1)
    specs = [
        pl.BlockSpec((depth, tile), lambda h, i, *_: (start // depth, jnp.where(h == 0, at(i), last))),
        pl.BlockSpec((depth, tile), lambda h, i, *_: (start // depth, jnp.where(h == 0, at(0), at(i)))),
        pl.BlockSpec((1, tile, 1), lambda h, i, *_: (h, at(i), 0)),
        pl.BlockSpec((1, tile, 1), lambda h, i, *_: (h, at(i), 0)),
    ]
    for near, _ in chunks:
        specs += [pl.BlockSpec((near.shape[0], wide), lambda h, i, *_: (0, 0))] * 2
    return specs


def paired(refs, count):
    return [(refs[2 * n], refs[2 * n + 1]) for n in range(count)]


def flat(chunks):
    return [one for pair in chunks for one in pair]


def accumulate(halves, perm, scale, chunks, start, total):
    tall = halves[0].shape[1]
    wide = chunks[0][0].shape[1]
    depth = sum(near.shape[0] for near, _ in chunks)
    tile = min(512, tall)
    count = len(chunks)

    def body(*refs):
        kept = refs[-2:]
        out = refs[-3]
        keep(paired(refs[4:], count), kept)
        result = tile_product(refs[:4], kept, pl.program_id(0), start)
        if total is not None:
            result = result + refs[-4][0]
        out[0] = result

    place = pl.BlockSpec((1, tile, wide), lambda h, i: (h, i, 0))
    specs = tile_specs(start, depth, chunks, tile, tall // tile, lambda i: i)
    operands = [*halves, perm, scale, *flat(chunks)]
    if total is not None:
        specs.append(place)
        operands.append(total)
    return pl.pallas_call(
        body,
        out_shape=jax.ShapeDtypeStruct((2, tall, wide), jnp.float32),
        grid=(2, tall // tile),
        in_specs=specs,
        out_specs=place,
        scratch_shapes=[pltpu.VMEM((depth, wide), jnp.bfloat16)] * 2,
        input_output_aliases={} if total is None else {len(operands) - 1: 0},
        compiler_params=pltpu.CompilerParams(vmem_limit_bytes=58 * 2**20),
        name="accumulate",
    )(*operands)


def finish(halves, perm, scale, chunks, start, total, features, origin):
    tall = halves[0].shape[1]
    wide = chunks[0][0].shape[1]
    depth = sum(near.shape[0] for near, _ in chunks)
    tile = min(512, tall)
    tiles = tall // tile
    count = len(chunks)

    def body(origin_ref, *refs):
        h = pl.program_id(0)
        total_ref, feature_ref, sim_ref, sum_ref, *kept = refs[4 + 2 * count :]
        keep(paired(refs[4:], count), kept)
        result = tile_product(refs[:4], kept, h, start) + total_ref[0]
        place = jnp.where(h == 0, origin_ref[0], 1 - origin_ref[0])
        row = origin_ref[1] + place * tall + pl.program_id(1) * tile
        row = row + lax.broadcasted_iota(jnp.int32, result.shape, 0)
        col = origin_ref[2] + lax.broadcasted_iota(jnp.int32, result.shape, 1)
        done = jnp.where(row == col, 1.0, decay_factor * result).astype(jnp.bfloat16)
        sim_ref[...] = done
        sum_ref[...] = dot(done, feature_ref[...])

    def placed(h, i, o):
        return (jnp.where(h == 0, o[0], 1 - o[0]) * tiles + i, 0)

    specs = tile_specs(start, depth, chunks, tile, tiles, lambda i: i)
    specs += [
        pl.BlockSpec((1, tile, wide), lambda h, i, o: (h, i, 0)),
        pl.BlockSpec(features.shape, lambda h, i, o: (0, 0)),
    ]
    operands = [*halves, perm, scale, *flat(chunks), total, features]
    return pl.pallas_call(
        body,
        out_shape=(
            jax.ShapeDtypeStruct((2 * tall, wide), jnp.bfloat16),
            jax.ShapeDtypeStruct((2 * tall, features.shape[1]), jnp.float32),
        ),
        grid_spec=pltpu.PrefetchScalarGridSpec(
            num_scalar_prefetch=1,
            grid=(2, tiles),
            in_specs=specs,
            out_specs=(
                pl.BlockSpec((tile, wide), placed),
                pl.BlockSpec((tile, features.shape[1]), placed),
            ),
            scratch_shapes=[pltpu.VMEM((depth, wide), jnp.bfloat16)] * 2,
        ),
        compiler_params=pltpu.CompilerParams(vmem_limit_bytes=58 * 2**20),
        name="finish",
    )(origin, *operands)


def gathered_block(diag_blocks, row_id, block_id, row_count, block_count):
    cols = 2 * block_count
    slice_rows = diag_blocks.shape[0] // row_count
    own = part(diag_blocks, row_id * slice_rows, slice_rows)
    ups, downs = [own], [own]
    for step in range(1, block_count):
        up_pairs = [(c, c + 2) for c in range(cols - 2) if c // 2 >= step - 1]
        down_pairs = [(c, c - 2) for c in range(2, cols) if c // 2 + step - 1 <= block_count - 1]
        ups.append(lax.ppermute(ups[-1], "col", up_pairs))
        downs.append(lax.ppermute(downs[-1], "col", down_pairs))
    slices = [own] + [ups[j] + downs[block_count - j] for j in range(1, block_count)]
    whole = jnp.zeros(diag_blocks.shape, diag_blocks.dtype)
    for distance in range(row_count):
        wanted = row_id ^ distance
        piece = pick(slices, (block_id - wanted) % block_count)
        if distance:
            piece = flipped(piece, "row", distance)
        whole = lax.dynamic_update_slice_in_dim(whole, piece, wanted * slice_rows, 0)
    return whole


def program(sim, diag_blocks, match_perm, match_scale, features):
    row_count = lax.axis_size("row")
    col_count = lax.axis_size("col")
    block_count = col_count // 2
    row_id = lax.axis_index("row")
    col_id = lax.axis_index("col")
    block_id = col_id // 2
    side = col_id % 2
    rows, half = sim.shape
    other = 1 - side
    bf16 = jnp.bfloat16
    spans = [(sum(parts[:n]) * rows // 16, parts[n] * rows // 16) for n in range(len(parts))]

    whole_b = gathered_block(diag_blocks, row_id, block_id, row_count, block_count)
    partner = flipped(sim, "col", 1)

    far_block = (block_id + block_count // 2) % block_count
    far_row = (row_id + row_count // 2) % row_count
    perm_c = part(lax.dynamic_index_in_dim(match_perm, far_block, 0, False), side * half, half)
    scale_c = part(lax.dynamic_index_in_dim(match_scale, far_block, 0, False), side * half, half)
    perm_r = lax.dynamic_index_in_dim(match_perm, far_row, 0, False)
    scale_r = lax.dynamic_index_in_dim(match_scale, far_row, 0, False)
    perm_r = jnp.stack([part(perm_r, side * half, half), part(perm_r, other * half, half)])
    scale_r = jnp.stack([part(scale_r, side * half, half), part(scale_r, other * half, half)])
    pick_own = one_hot(side * half, half, perm_c)
    pick_par = one_hot(other * half, half, perm_c)
    perm_r = perm_r[:, :, None]
    scale_r = scale_r[:, :, None]
    b_own = part(diag_blocks, side * half, half)
    b_par = part(diag_blocks, other * half, half)

    local = dot(sim, b_own)
    local = local + dot(partner, b_par)
    cuts = [sim[start : start + depth] for start, depth in spans]
    chunks = []
    for n, (start, depth) in enumerate(spans):
        span = slice(start, start + depth)
        got = shifted(cuts[n], "col", col_count // 2)
        got_par = flipped(got, "col", 1)
        moved = dot(got, pick_own) + dot(got_par, pick_par)
        mixed = (local[span] + moved * scale_c[None, :]).astype(bf16)
        chunks.append((mixed, shifted(mixed, "row", row_count // 2)))

    other_b = flipped(whole_b, "col", 1)
    halves = (whole_b, other_b)
    total = None
    for low, high in groups:
        total = accumulate(
            halves, perm_r, scale_r, chunks[low:high], spans[low][0], total
        )

    low = groups[-1][1]
    origin = jnp.stack([side, row_id * rows, col_id * half]).astype(jnp.int32)
    new_sim, sums = finish(
        halves, perm_r, scale_r, chunks[low:], spans[low][0], total,
        features, origin,
    )
    aggregated = scattered(sums, side, block_id, block_count)
    return new_sim, aggregated


def scattered(total, side, block_id, block_count):
    total = total.reshape(block_count, 2, -1, total.shape[1])
    kept = lax.dynamic_index_in_dim(total, side, 1, False)
    sent = lax.dynamic_index_in_dim(total, 1 - side, 1, False).astype(jnp.bfloat16)
    kept = kept + flipped(sent, "col", 1)
    result = lax.dynamic_index_in_dim(kept, block_id, 0, False)
    for distance in range(1, block_count):
        sent = lax.dynamic_index_in_dim(kept, block_id ^ distance, 0, False)
        result = result + flipped(sent.astype(jnp.bfloat16), "col", 2 * distance)
    return result


def solution(mesh):
    placed = (P("row", "col"), P(None, "col"), P(), P(), P("col", None))
    return jax.shard_map(
        program,
        mesh=mesh,
        in_specs=placed,
        out_specs=(P("row", "col"), P(("row", "col"), None)),
        check_vma=False,
    )
```

time: 505 us -> 394 us (0.78)
  waiting for transfers between devices: 375 us -> 198 us
  starting transfers between devices: 6.31 us -> 66.8 us
  Pallas kernels: 0 us -> 38.2 us
  matrix products: 29.8 us -> 60 us
  other arithmetic: 35.4 us -> 7.8 us
  local copies, waits for them, and re-layouts: 43.5 us -> 17.3 us
  between operations: 14.1 us -> 1.49 us
    ppermute x2 -> x18, waiting for transfers between devices: 285 us -> 153 us  [shifted(): return lax.ppermute(value, axis, pairs)]
    psum x1 -> x0, waiting for transfers between devices: 44.8 us -> none  [spread(): return lax.psum(jnp.where(mine, x, jnp.zeros_like(x)), axis)]
    ppermute x1 -> x24, waiting for transfers between devices: 5.5 us -> 44.8 us  [the longest x3 23.1 us: gathered_block(): downs.append(lax.ppermute(downs[-1], 'col', down_pairs))]
    reduce_scatter x1 -> x0, waiting for transfers between devices: 39.2 us -> none  [on_device(): lax.psum_scatter(partial_value, 'col', scatter_dimension=0, tiled=True)]
    pallas_call x0 -> x3, Pallas kernels: none -> 38.2 us  [the longest x2 25.6 us: accumulate(): pl.pallas_call(body, out_shape=jax.ShapeDtypeStruct((2, tall, wide), jnp....]
    ppermute x2 -> x18, starting transfers between devices: 5.56 us -> 41.1 us  [shifted(): return lax.ppermute(value, axis, pairs)]
    gather x3 -> x0, local copies, waits for them, and re-layouts: 33.4 us -> none  [the longest x2 19.7 us: on_device(): jnp.take(whole_block, own_perm, axis=1) * own_scale[None, :]]
    dot_general x4 -> x20, matrix products: 29.8 us -> 60 us  [dot(): return jnp.dot(a, b, preferred_element_type=jnp.float32)]
  transfers between devices with their start and end apart: 5 -> 42, of which waited for: 5 -> 21; matrix products, arithmetic and copies ran while one was open for 11% -> 20% of each run, Pallas kernels for 0% -> 7%
where the time goes in v1:
time: 394 us; the launch traced here: 389 us
  waiting for transfers between devices  198 us (50%)
  starting transfers between devices  66.8 us (17%)
  matrix products  60 us (15%)
  Pallas kernels  38.2 us (10%)
  local copies, waits for them, and re-layouts  17.3 us (4%)
  other arithmetic  7.8 us (2%)
    ppermute x18, waiting for transfers between devices, shifted(): return lax.ppermute(value, axis, pairs)  153 us
    dot_general x20, matrix products, dot(): return jnp.dot(a, b, preferred_element_type=jnp.float32)  60 us
    ppermute x18, starting transfers between devices, shifted(): return lax.ppermute(value, axis, pairs)  41.1 us
    pallas_call x2, Pallas kernels, accumulate(): pl.pallas_call(body, out_shape=jax.ShapeDtypeStruct((2, tall, wide), jnp....  25.6 us
    ppermute x3, waiting for transfers between devices, gathered_block(): downs.append(lax.ppermute(downs[-1], 'col', down_pairs))  23.1 us
    ppermute x18, waiting for transfers between devices, flipped(): return lax.ppermute(value, axis, pairs)  20.6 us
    pallas_call x1, Pallas kernels, finish(): pl.pallas_call(body, out_shape=(jax.ShapeDtypeStruct((2 * tall, wide), jn...  12.6 us
    ppermute x18, starting transfers between devices, flipped(): return lax.ppermute(value, axis, pairs)  12.6 us
  transfers between devices with their start and end apart: 42, of which 21 were waited for; matrix products, arithmetic and copies ran while one was open for 20% of the time, Pallas kernels for 7%

profile of v1, /device:TPU:0, one launch (start us, length us, event | category | flops | bytes accessed | tf_op | source)
XLA Modules:
  0.0 389.1 jit_solution(408121471354613655)
XLA Ops:
  0.6 1.3 constant_dynamic-slice_fusion
  1.9 1.3 collective-permute-start.3
  3.2 5.7 %collective-permute-start = (bf16[512,1024]{1,0:T(8,128)(2,1)S(1)}, bf16[512,1024]{1,0:T(8,128)(2,1)S(1)}, u32[]{:S(2)}, u32[]{:S(2)}) collective-permute-start(bf16[512,1024]{1,0:T(8,128)(2,1)S(1)} %constant_dynamic-slice_fusion), channel_id=1, source_target_pairs={{0,2},{1,3},{2,4},{3,5},{4,6},{5,7},{8,10},{9,11},{10,12},{11,13},... | collective-permute-start | bytes 3145736 | tf_op jit(solution)/shard_map/ppermute | solution.py:186
  9.0 3.9 fusion.218
  12.9 3.0 collective-permute-start.11
  15.9 14.2 %collective-permute-done.3 = bf16[512,1024]{1,0:T(8,128)(2,1)S(1)} collective-permute-done((bf16[512,1024]{1,0:T(8,128)(2,1)S(1)}, bf16[512,1024]{1,0:T(8,128)(2,1)S(1)}, u32[]{:S(2)}, u32[]{:S(2)}) %collective-permute-start.3) | collective-permute-done | bytes 1048608 | tf_op jit(solution)/shard_map/ppermute | solution.py:187
  30.0 1.3 collective-permute-start.4
  32.4 1.6 collective-permute-start.1
  34.0 1.8 fusion.219
  35.7 18.3 %collective-permute-start.14 = (bf16[128,1024]{1,0:T(8,128)(2,1)}, bf16[128,1024]{1,0:T(8,128)(2,1)}, u32[]{:S(2)}, u32[]{:S(2)}) collective-permute-start(bf16[128,1024]{1,0:T(8,128)(2,1)} %get-tuple-element.18), channel_id=1, source_target_pairs={{0,4},{1,5},{2,6},{3,7},{4,0},{5,1},{6,2},{7,3},{8,12},{9,13},{10,... | collective-permute-start | bytes 786440 | tf_op jit(solution)/shard_map/ppermute | solution.py:22
  54.1 10.7 %fusion.55 = f32[1024,2048]{0,1:T(8,128)} fusion(bf16[2048,1024]{1,0:T(8,128)(2,1)} %param.5, bf16[2048,1024]{1,0:T(8,128)(2,1)} %param.6, s32[]{:T(128)S(6)} %select_n.209), kind=kOutput, calls=%fused_computation.56 | convolution fusion | flops 4294967296 | bytes 14680068 | tf_op jit(solution)/shard_map/dot_general | solution.py:26
  65.8 2.0 collective-permute-done.4
  67.7 1.3 collective-permute-start.5
  69.0 2.0 collective-permute-start.2
  72.0 15.6 %collective-permute-done.14 = bf16[128,1024]{1,0:T(8,128)(2,1)} collective-permute-done((bf16[128,1024]{1,0:T(8,128)(2,1)}, bf16[128,1024]{1,0:T(8,128)(2,1)}, u32[]{:S(2)}, u32[]{:S(2)}) %collective-permute-start.14) | collective-permute-done | bytes 262176 | tf_op jit(solution)/shard_map/ppermute | solution.py:22
  87.6 3.0 collective-permute-start.17
  90.7 2.8 fusion.32
  93.4 8.1 %collective-permute-done.17 = bf16[128,1024]{1,0:T(8,128)(2,1)} collective-permute-done((bf16[128,1024]{1,0:T(8,128)(2,1)S(1)}, bf16[128,1024]{1,0:T(8,128)(2,1)}, u32[]{:S(2)}, u32[]{:S(2)}) %collective-permute-start.17) | collective-permute-done | bytes 262176 | tf_op jit(solution)/shard_map/ppermute | solution.py:22
  101.5 2.6 fusion.30
  104.2 2.9 collective-permute-start.23
  107.1 2.0 fusion.34
  109.1 7.0 %collective-permute-done.5 = bf16[512,1024]{1,0:T(8,128)(2,1)} collective-permute-done((bf16[512,1024]{1,0:T(8,128)(2,1)S(1)}, bf16[512,1024]{1,0:T(8,128)(2,1)}, u32[]{:S(2)}, u32[]{:S(2)}) %collective-permute-start.5) | collective-permute-done | bytes 1048608 | tf_op jit(solution)/shard_map/ppermute | solution.py:187
  116.1 3.7 select_select_fusion
  120.4 1.3 select_select_fusion.1
  121.7 1.6 collective-permute-start.6
  123.2 25.8 %collective-permute-done.20 = bf16[256,1024]{1,0:T(8,128)(2,1)S(1)} collective-permute-done((bf16[256,1024]{1,0:T(8,128)(2,1)}, bf16[256,1024]{1,0:T(8,128)(2,1)S(1)}, u32[]{:S(2)}, u32[]{:S(2)}) %collective-permute-start.20) | collective-permute-done | bytes 524320 | tf_op jit(solution)/shard_map/ppermute | solution.py:22
  149.0 1.5 collective-permute-start.7
  150.5 1.9 fusion.28
  152.4 7.8 %collective-permute-done.23 = bf16[256,1024]{1,0:T(8,128)(2,1)S(1)} collective-permute-done((bf16[256,1024]{1,0:T(8,128)(2,1)}, bf16[256,1024]{1,0:T(8,128)(2,1)S(1)}, u32[]{:S(2)}, u32[]{:S(2)}) %collective-permute-start.23) | collective-permute-done | bytes 524320 | tf_op jit(solution)/shard_map/ppermute | solution.py:22
  160.2 22.5 %collective-permute-done.26 = bf16[256,1024]{1,0:T(8,128)(2,1)S(1)} collective-permute-done((bf16[256,1024]{1,0:T(8,128)(2,1)S(1)}, bf16[256,1024]{1,0:T(8,128)(2,1)S(1)}, u32[]{:S(2)}, u32[]{:S(2)}) %collective-permute-start.26) | collective-permute-done | bytes 524320 | tf_op jit(solution)/shard_map/ppermute | solution.py:22
  182.7 2.4 collective-permute-start.8
  185.1 1.9 fusion.26
  187.1 1.9 fusion.24
  189.0 4.5 %collective-permute-done.29 = bf16[256,1024]{1,0:T(8,128)(2,1)S(1)} collective-permute-done((bf16[256,1024]{1,0:T(8,128)(2,1)S(1)}, bf16[256,1024]{1,0:T(8,128)(2,1)S(1)}, u32[]{:S(2)}, u32[]{:S(2)}) %collective-permute-start.29) | collective-permute-done | bytes 524320 | tf_op jit(solution)/shard_map/ppermute | solution.py:22
  194.5 3.0 collective-permute-start.35
  197.8 10.1 %collective-permute-done.8 = bf16[512,1024]{1,0:T(8,128)(2,1)S(1)} collective-permute-done((bf16[512,1024]{1,0:T(8,128)(2,1)S(1)}, bf16[512,1024]{1,0:T(8,128)(2,1)S(1)}, u32[]{:S(2)}, u32[]{:S(2)}) %collective-permute-start.8) | collective-permute-done | bytes 1048608 | tf_op jit(solution)/shard_map/ppermute | solution.py:16
  208.0 21.3 %collective-permute-done.32 = bf16[256,1024]{1,0:T(8,128)(2,1)S(1)} collective-permute-done((bf16[256,1024]{1,0:T(8,128)(2,1)S(1)}, bf16[256,1024]{1,0:T(8,128)(2,1)S(1)}, u32[]{:S(2)}, u32[]{:S(2)}) %collective-permute-start.32) | collective-permute-done | bytes 524320 | tf_op jit(solution)/shard_map/ppermute | solution.py:22
  229.4 13.1 %fusion.20 = f32[1024,256]{0,1:T(8,128)} fusion(bf16[256,1024]{1,0:T(8,128)(2,1)S(1)} %collective-permute-done.32, s32[1024]{0:T(1024)S(1)} %bitcast.115, s32[1024]{0:T(1024)S(1)} %iota_add_fusion.1), kind=kOutput, calls=%fused_computation.20 | convolution fusion | flops 537919488 | bytes 1581056 | tf_op jit(solution)/shard_map/dot_general | solution.py:26
  242.9 2.0 fusion.18
  244.9 11.0 %add_bitcast_fusion = f32[2048,1024]{1,0:T(8,128)S(1)} fusion(f32[1024,2048]{0,1:T(8,128)} %fusion.55, bf16[2048,1024]{1,0:T(8,128)(2,1)} %collective-permute-done.10, bf16[2048,1024]{1,0:T(8,128)(2,1)S(1)} %copy-done.2, s32[]{:T(128)S(6)} %select_n.211), kind=kOutput, calls=%fused_computation.36 | convolution fusion | flops 4297064448 | bytes 23068676 | tf_op jit(solution)/shard_map/dot_general | solution.py:26
  262.7 1.6 collective-permute-start.28
  265.9 1.5 collective-permute-start.34
  269.9 7.7 %collective-permute-done.28.refs_5_ = bf16[256,1024]{1,0:T(8,128)(2,1)S(1)} collective-permute-done((bf16[256,1024]{1,0:T(8,128)(2,1)S(1)}, bf16[256,1024]{1,0:T(8,128)(2,1)S(1)}, u32[]{:S(2)}, u32[]{:S(2)}) %collective-permute-start.28) | collective-permute-done | bytes 524320 | tf_op jit(solution)/shard_map/ppermute | solution.py:22
  277.6 1.5 collective-permute-start.13
  279.1 9.7 %collective-permute-done.31.refs_7_ = bf16[256,1024]{1,0:T(8,128)(2,1)S(1)} collective-permute-done((bf16[256,1024]{1,0:T(8,128)(2,1)S(1)}, bf16[256,1024]{1,0:T(8,128)(2,1)S(1)}, u32[]{:S(2)}, u32[]{:S(2)}) %collective-permute-start.31) | collective-permute-done | bytes 524320 | tf_op jit(solution)/shard_map/ppermute | solution.py:22
  288.9 1.5 collective-permute-start.22
  290.4 9.7 %collective-permute-done.34.refs_9_ = bf16[256,1024]{1,0:T(8,128)(2,1)S(1)} collective-permute-done((bf16[256,1024]{1,0:T(8,128)(2,1)S(1)}, bf16[256,1024]{1,0:T(8,128)(2,1)S(1)}, u32[]{:S(2)}, u32[]{:S(2)}) %collective-permute-start.34) | collective-permute-done | bytes 524320 | tf_op jit(solution)/shard_map/ppermute | solution.py:22
  300.1 1.5 collective-permute-start.25
  301.6 1.6 fusion.207.refs_8_
  303.2 8.1 %collective-permute-done.37.refs_11_ = bf16[256,1024]{1,0:T(8,128)(2,1)S(1)} collective-permute-done((bf16[256,1024]{1,0:T(8,128)(2,1)S(1)}, bf16[256,1024]{1,0:T(8,128)(2,1)S(1)}, u32[]{:S(2)}, u32[]{:S(2)}) %collective-permute-start.37) | collective-permute-done | bytes 524320 | tf_op jit(solution)/shard_map/ppermute | solution.py:22
  311.3 1.5 collective-permute-start.16
  312.8 2.0 copy-done.1
  315.3 1.4 copy.53.refs_2_
  316.7 1.4 copy.54.refs_3_
  318.7 14.4 %accumulate.2.refs_8_ = f32[2,1024,1024]{2,1,0:T(8,128)} custom-call(bf16[2048,1024]{1,0:T(8,128)(2,1)} %copy-done, bf16[2048,1024]{1,0:T(8,128)(2,1)} %copy-done.1, s32[2,1024,1]{2,1,0:T(8,128)} %copy.53.refs_2_, f32[2,1024,1]{2,1,0:T(8,128)} %copy.54.refs_3_, bf16[256,1024]{1,0:T(8,128)(2,1)} %copy-done.12, bf16[256,1024]{1,0:T(8,128)(2,1)} %copy-done.14, ...), custom_call_target="tpu_custom_call" | custom-call | tf_op jit(solution)/shard_map/accumulate/pallas_call | solution.py:114
  333.8 11.2 %collective-permute-done.25.refs_7_ = bf16[256,1024]{1,0:T(8,128)(2,1)S(1)} collective-permute-done((bf16[256,1024]{1,0:T(8,128)(2,1)S(1)}, bf16[256,1024]{1,0:T(8,128)(2,1)S(1)}, u32[]{:S(2)}, u32[]{:S(2)}) %collective-permute-start.25) | collective-permute-done | bytes 524320 | tf_op jit(solution)/shard_map/ppermute | solution.py:22
  345.8 11.2 %accumulate.3.refs_10_ = f32[2,1024,1024]{2,1,0:T(8,128)} custom-call(bf16[2048,1024]{1,0:T(8,128)(2,1)} %copy-done, bf16[2048,1024]{1,0:T(8,128)(2,1)} %copy-done.1, s32[2,1024,1]{2,1,0:T(8,128)} %copy.53.refs_2_, f32[2,1024,1]{2,1,0:T(8,128)} %copy.54.refs_3_, bf16[256,1024]{1,0:T(8,128)(2,1)} %copy-done.3, ...), custom_call_target="tpu_custom_call", output_to_operand_aliasing={{}: (8, {})} | custom-call | tf_op jit(solution)/shard_map/accumulate/pallas_call | solution.py:114
  357.9 12.6 %finish.1 = (bf16[2048,1024]{1,0:T(8,128)(2,1)}, f32[2048,256]{1,0:T(8,128)}) custom-call(s32[3]{0:T(128)} %pad_add_fusion.origin_ref, bf16[2048,1024]{1,0:T(8,128)(2,1)} %copy-done, bf16[2048,1024]{1,0:T(8,128)(2,1)} %copy-done.1, s32[2,1024,1]{2,1,0:T(8,128)} %copy.53.refs_2_, f32[2,1024,1]{2,1,0:T(8,128)} %copy.54.refs_3_, bf16[256,1024]{1,0:T(8,128)(2,1)} %copy-done.11, ...), custom_call_target="tpu_custom_call" | custom-call | tf_op jit(solution)/shard_map/finish/pallas_call | solution.py:157
  371.8 1.9 collective-permute-done.38
  373.7 1.3 bitcast_add_fusion
  375.1 2.4 collective-permute-start.41
  377.4 2.1 collective-permute-start.39
  379.5 3.9 %collective-permute-done.41 = bf16[256,256]{1,0:T(8,128)(2,1)S(1)} collective-permute-done((bf16[256,256]{1,0:T(8,128)(2,1)S(1)}, bf16[256,256]{1,0:T(8,128)(2,1)S(1)}, u32[]{:S(2)}, u32[]{:S(2)}) %collective-permute-start.41) | collective-permute-done | bytes 131104 | tf_op jit(solution)/shard_map/ppermute | solution.py:16
  383.4 4.7 %collective-permute-done.40 = bf16[256,256]{1,0:T(8,128)(2,1)S(1)} collective-permute-done((bf16[256,256]{1,0:T(8,128)(2,1)S(1)}, bf16[256,256]{1,0:T(8,128)(2,1)S(1)}, u32[]{:S(2)}, u32[]{:S(2)}) %collective-permute-start.40) | collective-permute-done | bytes 131104 | tf_op jit(solution)/shard_map/ppermute | solution.py:16
  (123 shorter events, 21.6 us)
Async XLA Ops:
  1.9 28.1 %collective-permute-start.3 = (bf16[512,1024]{1,0:T(8,128)(2,1)S(1)}, bf16[512,1024]{1,0:T(8,128)(2,1)S(1)}, u32[]{:S(2)}, u32[]{:S(2)}) collective-permute-start(bf16[512,1024]{1,0:T(8,128)(2,1)S(1)} %constant_dynamic-slice_fusion), channel_id=1, source_target_pairs={{2,0},{3,1},{4,2},{5,3},{6,4},{7,5},{10,8},{11,9},{12,10},{13,11},... | collective-permute-start | bytes 3145736 | tf_op jit(solution)/shard_map/ppermute | solution.py:187
  3.2 29.1 %collective-permute-start = (bf16[512,1024]{1,0:T(8,128)(2,1)S(1)}, bf16[512,1024]{1,0:T(8,128)(2,1)S(1)}, u32[]{:S(2)}, u32[]{:S(2)}) collective-permute-start(bf16[512,1024]{1,0:T(8,128)(2,1)S(1)} %constant_dynamic-slice_fusion), channel_id=1, source_target_pairs={{0,2},{1,3},{2,4},{3,5},{4,6},{5,7},{8,10},{9,11},{10,12},{11,13},... | collective-permute-start | bytes 3145736 | tf_op jit(solution)/shard_map/ppermute | solution.py:186
  8.9 236.0 %collective-permute-start.10 = (bf16[2048,1024]{1,0:T(8,128)(2,1)}, bf16[2048,1024]{1,0:T(8,128)(2,1)}, u32[]{:S(2)}, u32[]{:S(2)}) collective-permute-start(bf16[2048,1024]{1,0:T(8,128)(2,1)} %param.5), channel_id=1, source_target_pairs={{0,1},{1,0},{2,3},{3,2},{4,5},{5,4},{6,7},{7,6},{8,9},{9,8},{10,11... | collective-permute-start | bytes 12582920 | tf_op jit(solution)/shard_map/ppermute | solution.py:16
  12.9 91.3 %collective-permute-start.11 = (bf16[256,1024]{1,0:T(8,128)(2,1)}, bf16[256,1024]{1,0:T(8,128)(2,1)}, u32[]{:S(2)}, u32[]{:S(2)}) collective-permute-start(bf16[256,1024]{1,0:T(8,128)(2,1)} %get-tuple-element.15), channel_id=1, source_target_pairs={{0,4},{1,5},{2,6},{3,7},{4,0},{5,1},{6,2},{7,3},{8,12},{9,13},{10,... | collective-permute-start | bytes 1572872 | tf_op jit(solution)/shard_map/ppermute | solution.py:22
  30.0 37.7 %collective-permute-start.4 = (bf16[512,1024]{1,0:T(8,128)(2,1)S(1)}, bf16[512,1024]{1,0:T(8,128)(2,1)S(1)}, u32[]{:S(2)}, u32[]{:S(2)}) collective-permute-start(bf16[512,1024]{1,0:T(8,128)(2,1)S(1)} %collective-permute-done.3), channel_id=1, source_target_pairs={{2,0},{3,1},{4,2},{5,3},{10,8},{11,9},{12,10},{13,11},{18,16},{19,... | collective-permute-start | bytes 3145736 | tf_op jit(solution)/shard_map/ppermute | solution.py:187
  32.4 36.7 %collective-permute-start.1 = (bf16[512,1024]{1,0:T(8,128)(2,1)S(1)}, bf16[512,1024]{1,0:T(8,128)(2,1)}, u32[]{:S(2)}, u32[]{:S(2)}) collective-permute-start(bf16[512,1024]{1,0:T(8,128)(2,1)S(1)} %collective-permute-done), channel_id=1, source_target_pairs={{2,4},{3,5},{4,6},{5,7},{10,12},{11,13},{12,14},{13,15},{18,20},{1... | collective-permute-start | bytes 3145736 | tf_op jit(solution)/shard_map/ppermute | solution.py:186
  35.7 51.9 %collective-permute-start.14 = (bf16[128,1024]{1,0:T(8,128)(2,1)}, bf16[128,1024]{1,0:T(8,128)(2,1)}, u32[]{:S(2)}, u32[]{:S(2)}) collective-permute-start(bf16[128,1024]{1,0:T(8,128)(2,1)} %get-tuple-element.18), channel_id=1, source_target_pairs={{0,4},{1,5},{2,6},{3,7},{4,0},{5,1},{6,2},{7,3},{8,12},{9,13},{10,... | collective-permute-start | bytes 786440 | tf_op jit(solution)/shard_map/ppermute | solution.py:22
  67.7 48.3 %collective-permute-start.5 = (bf16[512,1024]{1,0:T(8,128)(2,1)S(1)}, bf16[512,1024]{1,0:T(8,128)(2,1)}, u32[]{:S(2)}, u32[]{:S(2)}) collective-permute-start(bf16[512,1024]{1,0:T(8,128)(2,1)S(1)} %collective-permute-done.4), channel_id=1, source_target_pairs={{2,0},{3,1},{10,8},{11,9},{18,16},{19,17},{26,24},{27,25}} | collective-permute-start | bytes 3145736 | tf_op jit(solution)/shard_map/ppermute | solution.py:187
  69.0 47.0 %collective-permute-start.2 = (bf16[512,1024]{1,0:T(8,128)(2,1)}, bf16[512,1024]{1,0:T(8,128)(2,1)}, u32[]{:S(2)}, u32[]{:S(2)}) collective-permute-start(bf16[512,1024]{1,0:T(8,128)(2,1)} %collective-permute-done.1), channel_id=1, source_target_pairs={{4,6},{5,7},{12,14},{13,15},{20,22},{21,23},{28,30},{29,31}} | collective-permute-start | bytes 3145736 | tf_op jit(solution)/shard_map/ppermute | solution.py:186
  87.6 13.9 %collective-permute-start.17 = (bf16[128,1024]{1,0:T(8,128)(2,1)S(1)}, bf16[128,1024]{1,0:T(8,128)(2,1)}, u32[]{:S(2)}, u32[]{:S(2)}) collective-permute-start(bf16[128,1024]{1,0:T(8,128)(2,1)S(1)} %get-tuple-element.17), channel_id=1, source_target_pairs={{0,4},{1,5},{2,6},{3,7},{4,0},{5,1},{6,2},{7,3},{8,12},{9,13},{10,... | collective-permute-start | bytes 786440 | tf_op jit(solution)/shard_map/ppermute | solution.py:22
  90.7 25.4 %copy-start.10 = (bf16[256,1024]{1,0:T(8,128)(2,1)S(1)}, bf16[256,1024]{1,0:T(8,128)(2,1)}, u32[]{:S(2)}) copy-start(bf16[256,1024]{1,0:T(8,128)(2,1)} %get-tuple-element.12) | copy-start | bytes 1572868
  90.7 25.4 %copy-start.2 = (bf16[2048,1024]{1,0:T(8,128)(2,1)S(1)}, bf16[2048,1024]{1,0:T(8,128)(2,1)}, u32[]{:S(2)}) copy-start(bf16[2048,1024]{1,0:T(8,128)(2,1)} %param.6) | copy-start | bytes 12582916
  101.5 47.4 %collective-permute-start.20 = (bf16[256,1024]{1,0:T(8,128)(2,1)}, bf16[256,1024]{1,0:T(8,128)(2,1)S(1)}, u32[]{:S(2)}, u32[]{:S(2)}) collective-permute-start(bf16[256,1024]{1,0:T(8,128)(2,1)} %get-tuple-element.14), channel_id=1, source_target_pairs={{0,4},{1,5},{2,6},{3,7},{4,0},{5,1},{6,2},{7,3},{8,12},{9,13},{10,... | collective-permute-start | bytes 1572872 | tf_op jit(solution)/shard_map/ppermute | solution.py:22
  104.2 56.1 %collective-permute-start.23 = (bf16[256,1024]{1,0:T(8,128)(2,1)}, bf16[256,1024]{1,0:T(8,128)(2,1)S(1)}, u32[]{:S(2)}, u32[]{:S(2)}) collective-permute-start(bf16[256,1024]{1,0:T(8,128)(2,1)} %get-tuple-element.13), channel_id=1, source_target_pairs={{0,4},{1,5},{2,6},{3,7},{4,0},{5,1},{6,2},{7,3},{8,12},{9,13},{10,... | collective-permute-start | bytes 1572872 | tf_op jit(solution)/shard_map/ppermute | solution.py:22
  116.1 66.6 %collective-permute-start.26 = (bf16[256,1024]{1,0:T(8,128)(2,1)S(1)}, bf16[256,1024]{1,0:T(8,128)(2,1)S(1)}, u32[]{:S(2)}, u32[]{:S(2)}) collective-permute-start(bf16[256,1024]{1,0:T(8,128)(2,1)S(1)} %copy-done.10), channel_id=1, source_target_pairs={{0,4},{1,5},{2,6},{3,7},{4,0},{5,1},{6,2},{7,3},{8,12},{9,13},{10,... | collective-permute-start | bytes 1572872 | tf_op jit(solution)/shard_map/ppermute | solution.py:22
  120.4 39.9 %copy-start.9 = (bf16[256,1024]{1,0:T(8,128)(2,1)S(1)}, bf16[256,1024]{1,0:T(8,128)(2,1)}, u32[]{:S(2)}) copy-start(bf16[256,1024]{1,0:T(8,128)(2,1)} %get-tuple-element.11) | copy-start | bytes 1572868
  121.7 72.8 %collective-permute-start.6 = (bf16[512,1024]{1,0:T(8,128)(2,1)S(1)}, bf16[512,1024]{1,0:T(8,128)(2,1)S(1)}, u32[]{:S(2)}, u32[]{:S(2)}) collective-permute-start(bf16[512,1024]{1,0:T(8,128)(2,1)S(1)} %get-tuple-element.20), channel_id=1, source_target_pairs={{0,8},{8,0},{16,24},{24,16},{1,9},{9,1},{17,25},{25,17},{2,10},{10... | collective-permute-start | bytes 3145736 | tf_op jit(solution)/shard_map/ppermute | solution.py:16
  149.0 48.6 %collective-permute-start.7 = (bf16[512,1024]{1,0:T(8,128)(2,1)S(1)}, bf16[512,1024]{1,0:T(8,128)(2,1)S(1)}, u32[]{:S(2)}, u32[]{:S(2)}) collective-permute-start(bf16[512,1024]{1,0:T(8,128)(2,1)S(1)} %get-tuple-element.19), channel_id=1, source_target_pairs={{0,16},{8,24},{16,0},{24,8},{1,17},{9,25},{17,1},{25,9},{2,18},{10... | collective-permute-start | bytes 3145736 | tf_op jit(solution)/shard_map/ppermute | solution.py:16
  152.4 41.1 %copy-start.8 = (bf16[256,1024]{1,0:T(8,128)(2,1)S(1)}, bf16[256,1024]{1,0:T(8,128)(2,1)}, u32[]{:S(2)}) copy-start(bf16[256,1024]{1,0:T(8,128)(2,1)} %get-tuple-element.16) | copy-start | bytes 1572868
  160.2 33.3 %collective-permute-start.29 = (bf16[256,1024]{1,0:T(8,128)(2,1)S(1)}, bf16[256,1024]{1,0:T(8,128)(2,1)S(1)}, u32[]{:S(2)}, u32[]{:S(2)}) collective-permute-start(bf16[256,1024]{1,0:T(8,128)(2,1)S(1)} %copy-done.9), channel_id=1, source_target_pairs={{0,4},{1,5},{2,6},{3,7},{4,0},{5,1},{6,2},{7,3},{8,12},{9,13},{10,... | collective-permute-start | bytes 1572872 | tf_op jit(solution)/shard_map/ppermute | solution.py:22
  182.7 25.2 %collective-permute-start.8 = (bf16[512,1024]{1,0:T(8,128)(2,1)S(1)}, bf16[512,1024]{1,0:T(8,128)(2,1)S(1)}, u32[]{:S(2)}, u32[]{:S(2)}) collective-permute-start(bf16[512,1024]{1,0:T(8,128)(2,1)S(1)} %get-tuple-element.6), channel_id=1, source_target_pairs={{0,24},{8,16},{16,8},{24,0},{1,25},{9,17},{17,9},{25,1},{2,26},{10... | collective-permute-start | bytes 3145736 | tf_op jit(solution)/shard_map/ppermute | solution.py:16
  187.1 7.4 %copy-start.7 = (bf16[256,1024]{1,0:T(8,128)(2,1)S(1)}, bf16[256,1024]{1,0:T(8,128)(2,1)}, u32[]{:S(2)}) copy-start(bf16[256,1024]{1,0:T(8,128)(2,1)} %get-tuple-element.10) | copy-start | bytes 1572868
  193.5 35.8 %collective-permute-start.32 = (bf16[256,1024]{1,0:T(8,128)(2,1)S(1)}, bf16[256,1024]{1,0:T(8,128)(2,1)S(1)}, u32[]{:S(2)}, u32[]{:S(2)}) collective-permute-start(bf16[256,1024]{1,0:T(8,128)(2,1)S(1)} %copy-done.8), channel_id=1, source_target_pairs={{0,4},{1,5},{2,6},{3,7},{4,0},{5,1},{6,2},{7,3},{8,12},{9,13},{10,... | collective-permute-start | bytes 1572872 | tf_op jit(solution)/shard_map/ppermute | solution.py:22
  194.5 47.9 %collective-permute-start.35 = (bf16[256,1024]{1,0:T(8,128)(2,1)S(1)}, bf16[256,1024]{1,0:T(8,128)(2,1)S(1)}, u32[]{:S(2)}, u32[]{:S(2)}) collective-permute-start(bf16[256,1024]{1,0:T(8,128)(2,1)S(1)} %copy-done.7), channel_id=1, source_target_pairs={{0,4},{1,5},{2,6},{3,7},{4,0},{5,1},{6,2},{7,3},{8,12},{9,13},{10,... | collective-permute-start | bytes 1572872 | tf_op jit(solution)/shard_map/ppermute | solution.py:22
  197.6 67.7 %collective-permute-start.15 = (bf16[128,1024]{1,0:T(8,128)(2,1)}, bf16[128,1024]{1,0:T(8,128)(2,1)S(1)}, u32[]{:S(2)}, u32[]{:S(2)}) collective-permute-start(bf16[128,1024]{1,0:T(8,128)(2,1)} %collective-permute-done.14), channel_id=1, source_target_pairs={{0,1},{1,0},{2,3},{3,2},{4,5},{5,4},{6,7},{7,6},{8,9},{9,8},{10,11... | collective-permute-start | bytes 786440 | tf_op jit(solution)/shard_map/ppermute | solution.py:16
  207.9 60.5 %collective-permute-start.18 = (bf16[128,1024]{1,0:T(8,128)(2,1)}, bf16[128,1024]{1,0:T(8,128)(2,1)S(1)}, u32[]{:S(2)}, u32[]{:S(2)}) collective-permute-start(bf16[128,1024]{1,0:T(8,128)(2,1)} %collective-permute-done.17), channel_id=1, source_target_pairs={{0,1},{1,0},{2,3},{3,2},{4,5},{5,4},{6,7},{7,6},{8,9},{9,8},{10,11... | collective-permute-start | bytes 786440 | tf_op jit(solution)/shard_map/ppermute | solution.py:16
  208.0 47.9 %copy-start = (bf16[2048,1024]{1,0:T(8,128)(2,1)}, bf16[2048,1024]{1,0:T(8,128)(2,1)S(1)}, u32[]{:S(2)}) copy-start(bf16[2048,1024]{1,0:T(8,128)(2,1)S(1)} %constant_dynamic-update-slice_fusion.refs_0_) | copy-start | bytes 12582916
  229.3 83.5 %collective-permute-start.9 = (bf16[2048,1024]{1,0:T(8,128)(2,1)S(1)}, bf16[2048,1024]{1,0:T(8,128)(2,1)S(1)}, u32[]{:S(2)}, u32[]{:S(2)}) collective-permute-start(bf16[2048,1024]{1,0:T(8,128)(2,1)S(1)} %constant_dynamic-update-slice_fusion.refs_0_), channel_id=1, source_target_pairs={{0,1},{1,0},{2,3},{3,2},{4,5},{5,4},{6,7},{7,6},{8,9},{9,8},{10,11... | collective-permute-start | bytes 12582920 | tf_op jit(solution)/shard_map/ppermute | solution.py:16
  242.4 13.5 %collective-permute-start.12 = (bf16[256,1024]{1,0:T(8,128)(2,1)}, bf16[256,1024]{1,0:T(8,128)(2,1)S(1)}, u32[]{:S(2)}, u32[]{:S(2)}) collective-permute-start(bf16[256,1024]{1,0:T(8,128)(2,1)} %collective-permute-done.11), channel_id=1, source_target_pairs={{0,1},{1,0},{2,3},{3,2},{4,5},{5,4},{6,7},{7,6},{8,9},{9,8},{10,11... | collective-permute-start | bytes 1572872 | tf_op jit(solution)/shard_map/ppermute | solution.py:16
  244.9 12.6 %collective-permute-start.21 = (bf16[256,1024]{1,0:T(8,128)(2,1)S(1)}, bf16[256,1024]{1,0:T(8,128)(2,1)S(1)}, u32[]{:S(2)}, u32[]{:S(2)}) collective-permute-start(bf16[256,1024]{1,0:T(8,128)(2,1)S(1)} %collective-permute-done.20), channel_id=1, source_target_pairs={{0,1},{1,0},{2,3},{3,2},{4,5},{5,4},{6,7},{7,6},{8,9},{9,8},{10,11... | collective-permute-start | bytes 1572872 | tf_op jit(solution)/shard_map/ppermute | solution.py:16
  256.0 2.6 collective-permute-start.24
  257.5 20.1 %copy-start.11 = (bf16[256,1024]{1,0:T(8,128)(2,1)}, bf16[256,1024]{1,0:T(8,128)(2,1)S(1)}, u32[]{:S(2)}) copy-start(bf16[256,1024]{1,0:T(8,128)(2,1)S(1)} %fusion.159.refs_4_) | copy-start | bytes 1572868
  257.5 2.6 collective-permute-start.27
  258.6 30.3 %copy-start.3 = (bf16[256,1024]{1,0:T(8,128)(2,1)}, bf16[256,1024]{1,0:T(8,128)(2,1)S(1)}, u32[]{:S(2)}) copy-start(bf16[256,1024]{1,0:T(8,128)(2,1)S(1)} %fusion.162.refs_4_) | copy-start | bytes 1572868
  258.6 2.6 collective-permute-start.30
  260.1 40.0 %copy-start.4 = (bf16[256,1024]{1,0:T(8,128)(2,1)}, bf16[256,1024]{1,0:T(8,128)(2,1)S(1)}, u32[]{:S(2)}) copy-start(bf16[256,1024]{1,0:T(8,128)(2,1)S(1)} %fusion.165.refs_6_) | copy-start | bytes 1572868
  260.1 4.2 %copy-start.26 = (f32[1024,256]{0,1:T(8,128)S(1)}, f32[1024,256]{0,1:T(8,128)}, u32[]{:S(2)}) copy-start(f32[1024,256]{0,1:T(8,128)} %fusion.20) | copy-start | bytes 3145732
  260.1 2.6 collective-permute-start.33
  261.2 4.1 %copy-start.12 = (bf16[256,1024]{1,0:T(8,128)(2,1)}, bf16[256,1024]{1,0:T(8,128)(2,1)S(1)}, u32[]{:S(2)}) copy-start(bf16[256,1024]{1,0:T(8,128)(2,1)S(1)} %fusion.168.refs_4_) | copy-start | bytes 1572868
  261.2 6.2 %copy-start.25 = (f32[1024,256]{0,1:T(8,128)S(1)}, f32[1024,256]{0,1:T(8,128)}, u32[]{:S(2)}) copy-start(f32[1024,256]{0,1:T(8,128)} %fusion.18) | copy-start | bytes 3145732
  261.2 4.7 %collective-permute-start.36 = (bf16[256,1024]{1,0:T(8,128)(2,1)S(1)}, bf16[256,1024]{1,0:T(8,128)(2,1)S(1)}, u32[]{:S(2)}, u32[]{:S(2)}) collective-permute-start(bf16[256,1024]{1,0:T(8,128)(2,1)S(1)} %collective-permute-done.35), channel_id=1, source_target_pairs={{0,1},{1,0},{2,3},{3,2},{4,5},{5,4},{6,7},{7,6},{8,9},{9,8},{10,11... | collective-permute-start | bytes 1572872 | tf_op jit(solution)/shard_map/ppermute | solution.py:16
  262.7 5.7 %copy-start.13 = (bf16[256,1024]{1,0:T(8,128)(2,1)}, bf16[256,1024]{1,0:T(8,128)(2,1)S(1)}, u32[]{:S(2)}) copy-start(bf16[256,1024]{1,0:T(8,128)(2,1)S(1)} %fusion.171.refs_6_) | copy-start | bytes 1572868
  262.7 6.3 %copy-start.28 = (f32[1024,128]{0,1:T(8,128)S(1)}, f32[1024,128]{0,1:T(8,128)}, u32[]{:S(2)}) copy-start(f32[1024,128]{0,1:T(8,128)} %fusion.32) | copy-start | bytes 1572868
  262.7 14.9 %collective-permute-start.28 = (bf16[256,1024]{1,0:T(8,128)(2,1)S(1)}, bf16[256,1024]{1,0:T(8,128)(2,1)S(1)}, u32[]{:S(2)}, u32[]{:S(2)}) collective-permute-start(bf16[256,1024]{1,0:T(8,128)(2,1)S(1)} %fusion.168.refs_4_), channel_id=1, source_target_pairs={{0,16},{8,24},{16,0},{24,8},{1,17},{9,25},{17,1},{25,9},{2,18},{10... | collective-permute-start | bytes 1572872 | tf_op jit(solution)/shard_map/ppermute | solution.py:22
  265.3 37.9 %copy-start.15 = (bf16[256,1024]{1,0:T(8,128)(2,1)}, bf16[256,1024]{1,0:T(8,128)(2,1)S(1)}, u32[]{:S(2)}) copy-start(bf16[256,1024]{1,0:T(8,128)(2,1)S(1)} %fusion.174.refs_8_) | copy-start | bytes 1572868
  265.3 36.3 %copy-start.27 = (f32[1024,128]{0,1:T(8,128)S(1)}, f32[1024,128]{0,1:T(8,128)}, u32[]{:S(2)}) copy-start(f32[1024,128]{0,1:T(8,128)} %fusion.30) | copy-start | bytes 1572868
  265.3 23.5 %collective-permute-start.31 = (bf16[256,1024]{1,0:T(8,128)(2,1)S(1)}, bf16[256,1024]{1,0:T(8,128)(2,1)S(1)}, u32[]{:S(2)}, u32[]{:S(2)}) collective-permute-start(bf16[256,1024]{1,0:T(8,128)(2,1)S(1)} %fusion.171.refs_6_), channel_id=1, source_target_pairs={{0,16},{8,24},{16,0},{24,8},{1,17},{9,25},{17,1},{25,9},{2,18},{10... | collective-permute-start | bytes 1572872 | tf_op jit(solution)/shard_map/ppermute | solution.py:22
  265.9 34.2 %collective-permute-start.34 = (bf16[256,1024]{1,0:T(8,128)(2,1)S(1)}, bf16[256,1024]{1,0:T(8,128)(2,1)S(1)}, u32[]{:S(2)}, u32[]{:S(2)}) collective-permute-start(bf16[256,1024]{1,0:T(8,128)(2,1)S(1)} %fusion.174.refs_8_), channel_id=1, source_target_pairs={{0,16},{8,24},{16,0},{24,8},{1,17},{9,25},{17,1},{25,9},{2,18},{10... | collective-permute-start | bytes 1572872 | tf_op jit(solution)/shard_map/ppermute | solution.py:22
  268.4 46.9 %copy-start.19 = (bf16[256,1024]{1,0:T(8,128)(2,1)}, bf16[256,1024]{1,0:T(8,128)(2,1)S(1)}, u32[]{:S(2)}) copy-start(bf16[256,1024]{1,0:T(8,128)(2,1)S(1)} %fusion.177.refs_10_) | copy-start | bytes 1572868
  268.4 42.9 %collective-permute-start.37 = (bf16[256,1024]{1,0:T(8,128)(2,1)S(1)}, bf16[256,1024]{1,0:T(8,128)(2,1)S(1)}, u32[]{:S(2)}, u32[]{:S(2)}) collective-permute-start(bf16[256,1024]{1,0:T(8,128)(2,1)S(1)} %fusion.177.refs_10_), channel_id=1, source_target_pairs={{0,16},{8,24},{16,0},{24,8},{1,17},{9,25},{17,1},{25,9},{2,18},{10... | collective-permute-start | bytes 1572872 | tf_op jit(solution)/shard_map/ppermute | solution.py:22
  269.9 63.3 %copy-start.21 = (bf16[128,1024]{1,0:T(8,128)(2,1)}, bf16[128,1024]{1,0:T(8,128)(2,1)S(1)}, u32[]{:S(2)}) copy-start(bf16[128,1024]{1,0:T(8,128)(2,1)S(1)} %fusion.204.refs_6_) | copy-start | bytes 786436
  277.6 12.8 %copy-start.14 = (bf16[256,1024]{1,0:T(8,128)(2,1)}, bf16[256,1024]{1,0:T(8,128)(2,1)S(1)}, u32[]{:S(2)}) copy-start(bf16[256,1024]{1,0:T(8,128)(2,1)S(1)} %collective-permute-done.28.refs_5_) | copy-start | bytes 1572868
  277.6 79.4 %collective-permute-start.13 = (bf16[256,1024]{1,0:T(8,128)(2,1)S(1)}, bf16[256,1024]{1,0:T(8,128)(2,1)S(1)}, u32[]{:S(2)}, u32[]{:S(2)}) collective-permute-start(bf16[256,1024]{1,0:T(8,128)(2,1)S(1)} %fusion.159.refs_4_), channel_id=1, source_target_pairs={{0,16},{8,24},{16,0},{24,8},{1,17},{9,25},{17,1},{25,9},{2,18},{10... | collective-permute-start | bytes 1572872 | tf_op jit(solution)/shard_map/ppermute | solution.py:22
  288.8 26.5 %copy-start.17 = (bf16[256,1024]{1,0:T(8,128)(2,1)}, bf16[256,1024]{1,0:T(8,128)(2,1)S(1)}, u32[]{:S(2)}) copy-start(bf16[256,1024]{1,0:T(8,128)(2,1)S(1)} %collective-permute-done.31.refs_7_) | copy-start | bytes 1572868
  288.9 44.9 %collective-permute-start.22 = (bf16[256,1024]{1,0:T(8,128)(2,1)S(1)}, bf16[256,1024]{1,0:T(8,128)(2,1)S(1)}, u32[]{:S(2)}, u32[]{:S(2)}) collective-permute-start(bf16[256,1024]{1,0:T(8,128)(2,1)S(1)} %fusion.162.refs_4_), channel_id=1, source_target_pairs={{0,16},{8,24},{16,0},{24,8},{1,17},{9,25},{17,1},{25,9},{2,18},{10... | collective-permute-start | bytes 1572872 | tf_op jit(solution)/shard_map/ppermute | solution.py:22
  300.1 15.2 %copy-start.18 = (bf16[256,1024]{1,0:T(8,128)(2,1)}, bf16[256,1024]{1,0:T(8,128)(2,1)S(1)}, u32[]{:S(2)}) copy-start(bf16[256,1024]{1,0:T(8,128)(2,1)S(1)} %collective-permute-done.34.refs_9_) | copy-start | bytes 1572868
  300.1 44.9 %collective-permute-start.25 = (bf16[256,1024]{1,0:T(8,128)(2,1)S(1)}, bf16[256,1024]{1,0:T(8,128)(2,1)S(1)}, u32[]{:S(2)}, u32[]{:S(2)}) collective-permute-start(bf16[256,1024]{1,0:T(8,128)(2,1)S(1)} %fusion.165.refs_6_), channel_id=1, source_target_pairs={{0,16},{8,24},{16,0},{24,8},{1,17},{9,25},{17,1},{25,9},{2,18},{10... | collective-permute-start | bytes 1572872 | tf_op jit(solution)/shard_map/ppermute | solution.py:22
  311.3 45.7 %collective-permute-start.16 = (bf16[128,1024]{1,0:T(8,128)(2,1)S(1)}, bf16[128,1024]{1,0:T(8,128)(2,1)}, u32[]{:S(2)}, u32[]{:S(2)}) collective-permute-start(bf16[128,1024]{1,0:T(8,128)(2,1)S(1)} %fusion.204.refs_6_), channel_id=1, source_target_pairs={{0,16},{8,24},{16,0},{24,8},{1,17},{9,25},{17,1},{25,9},{2,18},{10... | collective-permute-start | bytes 786440 | tf_op jit(solution)/shard_map/ppermute | solution.py:22
  314.8 42.2 %collective-permute-start.19 = (bf16[128,1024]{1,0:T(8,128)(2,1)}, bf16[128,1024]{1,0:T(8,128)(2,1)}, u32[]{:S(2)}, u32[]{:S(2)}) collective-permute-start(bf16[128,1024]{1,0:T(8,128)(2,1)} %fusion.207.refs_8_), channel_id=1, source_target_pairs={{0,16},{8,24},{16,0},{24,8},{1,17},{9,25},{17,1},{25,9},{2,18},{10... | collective-permute-start | bytes 786440 | tf_op jit(solution)/shard_map/ppermute | solution.py:22
  333.8 11.2 %copy-start.5 = (bf16[256,1024]{1,0:T(8,128)(2,1)}, bf16[256,1024]{1,0:T(8,128)(2,1)S(1)}, u32[]{:S(2)}) copy-start(bf16[256,1024]{1,0:T(8,128)(2,1)S(1)} %collective-permute-done.22.refs_5_) | copy-start | bytes 1572868
  371.7 2.0 collective-permute-start.38
  375.1 8.4 %collective-permute-start.41 = (bf16[256,256]{1,0:T(8,128)(2,1)S(1)}, bf16[256,256]{1,0:T(8,128)(2,1)S(1)}, u32[]{:S(2)}, u32[]{:S(2)}) collective-permute-start(bf16[256,256]{1,0:T(8,128)(2,1)S(1)} %get-tuple-element.23), channel_id=1, source_target_pairs={{0,6},{1,7},{2,4},{3,5},{4,2},{5,3},{6,0},{7,1},{8,14},{9,15},{10,... | collective-permute-start | bytes 393224 | tf_op jit(solution)/shard_map/ppermute | solution.py:16
  377.4 10.7 %collective-permute-start.40 = (bf16[256,256]{1,0:T(8,128)(2,1)S(1)}, bf16[256,256]{1,0:T(8,128)(2,1)S(1)}, u32[]{:S(2)}, u32[]{:S(2)}) collective-permute-start(bf16[256,256]{1,0:T(8,128)(2,1)S(1)} %get-tuple-element.24), channel_id=1, source_target_pairs={{0,4},{1,5},{2,6},{3,7},{4,0},{5,1},{6,2},{7,3},{8,12},{9,13},{10,... | collective-permute-start | bytes 393224 | tf_op jit(solution)/shard_map/ppermute | solution.py:16
  377.4 10.7 %collective-permute-start.39 = (bf16[256,256]{1,0:T(8,128)(2,1)S(1)}, bf16[256,256]{1,0:T(8,128)(2,1)S(1)}, u32[]{:S(2)}, u32[]{:S(2)}) collective-permute-start(bf16[256,256]{1,0:T(8,128)(2,1)S(1)} %get-tuple-element.22), channel_id=1, source_target_pairs={{0,2},{1,3},{2,0},{3,1},{4,6},{5,7},{6,4},{7,5},{8,10},{9,11},{10,... | collective-permute-start | bytes 393224 | tf_op jit(solution)/shard_map/ppermute | solution.py:16
  (7 other events, 14.6 us)
